TPU v7x, 32 devices: a whole 2x2x4 slice. The times are simulated.
32 devices in a mesh: seq: 8 (over z, y), tok: 4 (over x, core).
Axes of the slice: x: 2, y: 2, z: 4, core: 2. Of those that a mesh axis runs over, the one named last changes fastest.
Arguments:
- tokens: bfloat16 [8, 1024, 1024], P('seq', 'tok'), may hold values from -6 to 6
- out_grad: bfloat16 [8, 1024, 1024], P('seq', 'tok'), may hold values from -6 to 6
- segments: int32 [8, 1024], P('seq'), may hold values from 0 to 2, never falling along the last dimension, each value on 1 to 512 neighbouring positions
- adapter_index: int32 [8], P('seq'), may hold values from 0 to 7
- qkv_weight: bfloat16 [1024, 3072], P('tok', 'seq'), may hold values from -0.1875 to 0.1875
- out_weight: bfloat16 [1024, 1024], P('tok', 'seq'), may hold values from -0.75 to 0.75
- in_weight: bfloat16 [1024, 5248], P('tok', 'seq'), may hold values from -0.1875 to 0.1875
- out2_weight: bfloat16 [2624, 1024], P('tok', 'seq'), may hold values from -0.15625 to 0.15625
- attn_gain: bfloat16 [1024], P('tok'), may hold values from 0.099609375 to 1.8984375
- mlp_gain: bfloat16 [1024], P('tok'), may hold values from 0.099609375 to 1.8984375
- qkv_down: bfloat16 [8, 16, 1024], replicated, may hold values from -0.1875 to 0.1875
- qkv_up: bfloat16 [8, 16, 3072], replicated, may hold values from -0.5 to 0.5
- out_down: bfloat16 [8, 16, 1024], replicated, may hold values from -0.1875 to 0.1875
- out_up: bfloat16 [8, 16, 1024], replicated, may hold values from -1.5 to 1.5
- in_down: bfloat16 [8, 16, 1024], replicated, may hold values from -0.1875 to 0.1875
- in_up: bfloat16 [8, 16, 5248], replicated, may hold values from -0.5 to 0.5
- out2_down: bfloat16 [8, 16, 2624], replicated, may hold values from -0.125 to 0.125
- out2_up: bfloat16 [8, 16, 1024], replicated, may hold values from -0.5 to 0.5
Outputs:
- layer_out: bfloat16 [8, 1024, 1024], P('seq', 'tok')
- input_grad: bfloat16 [8, 1024, 1024], P('seq', 'tok')
- qkv_down_grad: float32 [8, 16, 1024], replicated
- qkv_up_grad: float32 [8, 16, 3072], replicated
- out_down_grad: float32 [8, 16, 1024], replicated
- out_up_grad: float32 [8, 16, 1024], replicated
- in_down_grad: float32 [8, 16, 1024], replicated
- in_up_grad: float32 [8, 16, 5248], replicated
- out2_down_grad: float32 [8, 16, 2624], replicated
- out2_up_grad: float32 [8, 16, 1024], replicated
Inputs may be any that keep to these rules, and one draw needn't show every extreme that they name: `segments`: within a sequence the document numbers never fall; each document has 1 to 512 tokens, one of each sequence exactly 512.
All inputs are finite; a program needn't handle non-finite values.
Results may differ from a plain program's by a relative error of at most 0.018.
Values may be sent and summed in bfloat16 or wider, within the bound.
No kernel may reach another device: no remote copies, remote signals or barrier semaphores. Data moves between devices by JAX's collectives and lax.ppermute only.
A program may use at most 128 MiB of HBM per device.

v0:
```python
import jax
import jax.numpy as jnp
from jax import lax
from jax.sharding import PartitionSpec as P

HEADS = 16
HEAD_DIM = 64
FF = 2624
ADAPTERS = 8
EPS = 1e-05
THETA = 160000.0
HIGH = lax.Precision.HIGHEST


def layer_norm(values, gain_vec):
    middle = jnp.mean(values, axis=-1, keepdims=True)
    centered = values - middle
    spread = jnp.mean(centered * centered, axis=-1, keepdims=True)
    return centered * lax.rsqrt(spread + EPS) * gain_vec


def rotary_table(positions, head_width):
    exponent = jnp.arange(0, head_width, 2).astype(jnp.float32) / head_width
    inverse = 1.0 / THETA**exponent
    phases = positions.astype(jnp.float32)[:, None] * inverse[None, :]
    cosine = jnp.concatenate([jnp.cos(phases), jnp.cos(phases)], -1)
    sine_part = jnp.concatenate([jnp.sin(phases), jnp.sin(phases)], -1)
    return (cosine, sine_part)


def rotary(values, cosine, sine_part):
    half_width = values.shape[-1] // 2
    turned = jnp.concatenate([-values[..., half_width:], values[..., :half_width]], -1)
    return values * cosine[None, :, None, :] + turned * sine_part[None, :, None, :]


def glu_act(inputs, gate_vals):
    return jax.nn.gelu(inputs, approximate=False) * gate_vals


def select(table_rows, onehot_low):
    return jnp.einsum(
        "sa,ayz->syz", onehot_low, table_rows, preferred_element_type=jnp.float32
    ).astype(jnp.bfloat16)


def spread_back(term_rows, onehot):
    return jnp.einsum(
        "sa,syz->ayz", onehot, term_rows, precision=HIGH, preferred_element_type=jnp.float32
    )


def project(inputs, weight, down_rows, up_rows):
    seq_count, row_count, width_in = inputs.shape
    main_part = jnp.dot(
        inputs.reshape(seq_count * row_count, width_in), weight, preferred_element_type=jnp.float32
    )
    narrow = jnp.einsum(
        "std,srd->str", inputs, down_rows, preferred_element_type=jnp.float32
    ).astype(jnp.bfloat16)
    extra_part = jnp.einsum("str,sre->ste", narrow, up_rows, preferred_element_type=jnp.float32)
    return (main_part.reshape(seq_count, row_count, -1) + extra_part, narrow)


def project_back(grad_out, inputs, narrow, weight, down_rows, up_rows):
    seq_count, row_count, width_out = grad_out.shape
    main_part = lax.dot_general(
        grad_out.reshape(seq_count * row_count, width_out),
        weight,
        (((1,), (1,)), ((), ())),
        preferred_element_type=jnp.float32,
    )
    inner_grad = jnp.einsum(
        "ste,sre->str", grad_out, up_rows, preferred_element_type=jnp.float32
    ).astype(jnp.bfloat16)
    back_sum = main_part.reshape(seq_count, row_count, -1) + jnp.einsum(
        "str,srd->std", inner_grad, down_rows, preferred_element_type=jnp.float32
    )
    grad_up = jnp.einsum("str,ste->sre", narrow, grad_out, preferred_element_type=jnp.float32)
    grad_down = jnp.einsum("str,std->srd", inner_grad, inputs, preferred_element_type=jnp.float32)
    return (back_sum, grad_down, grad_up)


def masked_scores(query_part, key_part, doc_mask):
    scores = (
        jnp.einsum("sqhd,skhd->shqk", query_part, key_part, preferred_element_type=jnp.float32)
        * 0.125
    )
    return jnp.where(doc_mask[:, None, :, :], scores, -1e30)


def heads_slice(source, group_index, group_width, head_width):
    part_cols = lax.dynamic_slice_in_dim(source, group_index * group_width, group_width, 2)
    return part_cols.reshape(
        part_cols.shape[0], part_cols.shape[1], group_width // head_width, head_width
    )


def join_groups(parts):
    moved = jnp.moveaxis(parts, 0, 2)
    return moved.reshape(moved.shape[0], moved.shape[1], -1)


def body(
    tokens,
    out_grad,
    segments,
    adapter_index,
    qkv_weight,
    out_weight,
    in_weight,
    out2_weight,
    attn_gain,
    mlp_gain,
    qkv_down,
    qkv_up,
    out_down,
    out_up,
    in_down,
    in_up,
    out2_down,
    out2_up,
):
    seq_count, tok_rows, model_width = tokens.shape
    head_width = HEAD_DIM
    group_width = 2 * head_width
    groups = jnp.arange(HEADS // 2)
    seq_length = segments.shape[1]
    tok_start = lax.axis_index("tok") * tok_rows
    positions = tok_start + jnp.arange(tok_rows)
    cosine, sine_part = rotary_table(positions, head_width)
    own_segments = lax.dynamic_slice_in_dim(segments, tok_start, tok_rows, 1)
    doc_mask = own_segments[:, :, None] == segments[:, None, :]
    pick_bits = adapter_index[:, None] == jnp.arange(ADAPTERS)[None, :]
    onehot = pick_bits.astype(jnp.float32)
    onehot_low = pick_bits.astype(jnp.bfloat16)
    picked = [
        select(table_rows, onehot_low)
        for table_rows in (qkv_down, qkv_up, out_down, out_up, in_down, in_up, out2_down, out2_up)
    ]
    tok_parts = (
        lax.all_gather(qkv_weight, "tok", axis=0, tiled=True),
        lax.all_gather(out_weight, "tok", axis=0, tiled=True),
        lax.all_gather(in_weight, "tok", axis=0, tiled=True),
        lax.all_gather(out2_weight, "tok", axis=0, tiled=True),
        lax.all_gather(attn_gain, "tok", axis=0, tiled=True),
        lax.all_gather(mlp_gain, "tok", axis=0, tiled=True),
    )
    w_qkv, w_out, w_in, w_out2 = (
        lax.all_gather(tok_parts[0], "seq", axis=1, tiled=True),
        lax.all_gather(tok_parts[1], "seq", axis=1, tiled=True),
        lax.all_gather(tok_parts[2], "seq", axis=1, tiled=True),
        lax.all_gather(tok_parts[3], "seq", axis=1, tiled=True),
    )
    gain_one = tok_parts[4].astype(jnp.float32)
    gain_two = tok_parts[5].astype(jnp.float32)
    inputs = tokens.astype(jnp.float32)
    norm_one = layer_norm(inputs, gain_one).astype(jnp.bfloat16)
    qkv, narrow_qkv = project(norm_one, w_qkv, picked[0], picked[1])
    head_shape = (seq_count, tok_rows, HEADS, head_width)
    query_pre = qkv[..., :model_width].reshape(head_shape)
    query_low = (
        rotary(query_pre, cosine, sine_part)
        .reshape(seq_count, tok_rows, model_width)
        .astype(jnp.bfloat16)
    )
    key_low = (
        rotary(qkv[..., model_width : 2 * model_width].reshape(head_shape), cosine, sine_part)
        .reshape(seq_count, tok_rows, model_width)
        .astype(jnp.bfloat16)
    )
    value_low = qkv[..., 2 * model_width :].astype(jnp.bfloat16)
    keys_all, values_all = (
        lax.all_gather(key_low, "tok", axis=1, tiled=True),
        lax.all_gather(value_low, "tok", axis=1, tiled=True),
    )

    def forward_group(group_index):
        query_part = heads_slice(query_low, group_index, group_width, head_width)
        key_part = heads_slice(keys_all, group_index, group_width, head_width)
        value_part = heads_slice(values_all, group_index, group_width, head_width)
        scores = masked_scores(query_part, key_part, doc_mask)
        row_max = jnp.max(scores, axis=-1, keepdims=True)
        row_total = jnp.sum(jnp.exp(scores - row_max), axis=-1, keepdims=True)
        log_total = row_max + jnp.log(row_total)
        attn_prob = jnp.exp(scores - log_total).astype(jnp.bfloat16)
        mixed = jnp.einsum(
            "shqk,skhd->sqhd", attn_prob, value_part, preferred_element_type=jnp.float32
        )
        return (mixed.reshape(seq_count, tok_rows, group_width), log_total[..., 0])

    mixed_parts, log_totals = lax.map(forward_group, groups)
    attn_low = join_groups(mixed_parts).astype(jnp.bfloat16)
    attn_branch, narrow_out = project(attn_low, w_out, picked[2], picked[3])
    middle = inputs + attn_branch
    norm_two = layer_norm(middle, gain_two).astype(jnp.bfloat16)
    gate_up, narrow_in = project(norm_two, w_in, picked[4], picked[5])
    act_low = glu_act(gate_up[..., :FF], gate_up[..., FF:]).astype(jnp.bfloat16)
    mlp_branch, narrow_out2 = project(act_low, w_out2, picked[6], picked[7])
    layer_out = (middle + mlp_branch).astype(jnp.bfloat16)
    back_parts = (
        lax.all_gather(qkv_weight, "tok", axis=0, tiled=True),
        lax.all_gather(out_weight, "tok", axis=0, tiled=True),
        lax.all_gather(in_weight, "tok", axis=0, tiled=True),
        lax.all_gather(out2_weight, "tok", axis=0, tiled=True),
    )
    w_qkv, w_out, w_in, w_out2 = (
        lax.all_gather(back_parts[0], "seq", axis=1, tiled=True),
        lax.all_gather(back_parts[1], "seq", axis=1, tiled=True),
        lax.all_gather(back_parts[2], "seq", axis=1, tiled=True),
        lax.all_gather(back_parts[3], "seq", axis=1, tiled=True),
    )
    grad_y = out_grad.astype(jnp.float32)
    back_act, down_o2, up_o2 = project_back(
        out_grad, act_low, narrow_out2, w_out2, picked[6], picked[7]
    )
    _, glu_back = jax.vjp(glu_act, gate_up[..., :FF], gate_up[..., FF:])
    grad_in, grad_gate = glu_back(back_act)
    grad_z = jnp.concatenate([grad_in, grad_gate], axis=-1).astype(jnp.bfloat16)
    back_norm_two, down_in, up_in = project_back(
        grad_z, norm_two, narrow_in, w_in, picked[4], picked[5]
    )
    _, norm_two_back = jax.vjp(lambda field: layer_norm(field, gain_two), middle)
    grad_mid = grad_y + norm_two_back(back_norm_two)[0]
    grad_a = grad_mid.astype(jnp.bfloat16)
    back_attn, down_out, up_out = project_back(
        grad_a, attn_low, narrow_out, w_out, picked[2], picked[3]
    )
    grad_attn = back_attn.astype(jnp.bfloat16)

    def query_grads(group_index):
        query_part = heads_slice(query_low, group_index, group_width, head_width)
        key_part = heads_slice(keys_all, group_index, group_width, head_width)
        value_part = heads_slice(values_all, group_index, group_width, head_width)
        grad_part = heads_slice(grad_attn, group_index, group_width, head_width)
        scores = masked_scores(query_part, key_part, doc_mask)
        attn_prob = jnp.exp(scores - log_totals[group_index][..., None])
        grad_prob = jnp.einsum(
            "sqhd,skhd->shqk", grad_part, value_part, preferred_element_type=jnp.float32
        )
        row_dot = jnp.sum(attn_prob * grad_prob, axis=-1)
        grad_scores = (attn_prob * (grad_prob - row_dot[..., None]) * 0.125).astype(jnp.bfloat16)
        grad_query = jnp.einsum(
            "shqk,skhd->sqhd", grad_scores, key_part, preferred_element_type=jnp.float32
        )
        return (
            query_part,
            grad_part,
            attn_prob,
            grad_scores,
            grad_query.reshape(seq_count, tok_rows, group_width),
            row_dot,
        )

    def summed_group(group_index):
        query_part, grad_part, attn_prob, grad_scores, grad_query, row_dot = query_grads(
            group_index
        )
        grad_key = jnp.einsum(
            "shqk,sqhd->skhd", grad_scores, query_part, preferred_element_type=jnp.float32
        )
        grad_value = jnp.einsum(
            "shqk,sqhd->skhd",
            attn_prob.astype(jnp.bfloat16),
            grad_part,
            preferred_element_type=jnp.float32,
        )
        grad_key, grad_value = (
            lax.psum_scatter(
                grad_key.reshape(seq_count, seq_length, group_width).astype(jnp.bfloat16),
                "tok",
                scatter_dimension=1,
                tiled=True,
            ).astype(jnp.float32),
            lax.psum_scatter(
                grad_value.reshape(seq_count, seq_length, group_width).astype(jnp.bfloat16),
                "tok",
                scatter_dimension=1,
                tiled=True,
            ).astype(jnp.float32),
        )
        return (grad_query, grad_key, grad_value)

    query_parts, key_parts, value_parts = lax.map(summed_group, groups)
    grad_query = join_groups(query_parts)
    grad_key = join_groups(key_parts)
    grad_value = join_groups(value_parts)
    _, rotate_back = jax.vjp(lambda field: rotary(field, cosine, sine_part), query_pre)
    grad_query_pre = rotate_back(grad_query.reshape(head_shape))[0].reshape(
        seq_count, tok_rows, model_width
    )
    grad_key_pre = rotate_back(grad_key.reshape(head_shape))[0].reshape(
        seq_count, tok_rows, model_width
    )
    grad_qkv = jnp.concatenate([grad_query_pre, grad_key_pre, grad_value], axis=-1).astype(
        jnp.bfloat16
    )
    back_norm_one, down_qkv, up_qkv = project_back(
        grad_qkv, norm_one, narrow_qkv, w_qkv, picked[0], picked[1]
    )
    _, norm_one_back = jax.vjp(lambda field: layer_norm(field, gain_one), inputs)
    input_grad = (grad_mid + norm_one_back(back_norm_one)[0]).astype(jnp.bfloat16)
    terms = (down_qkv, up_qkv, down_out, up_out, down_in, up_in, down_o2, up_o2)
    summed = lax.psum(
        (
            spread_back(terms[0], onehot),
            spread_back(terms[1], onehot),
            spread_back(terms[2], onehot),
            spread_back(terms[3], onehot),
            spread_back(terms[4], onehot),
            spread_back(terms[5], onehot),
            spread_back(terms[6], onehot),
            spread_back(terms[7], onehot),
        ),
        ("seq", "tok"),
    )
    return (
        layer_out,
        input_grad,
        summed[0],
        summed[1],
        summed[2],
        summed[3],
        summed[4],
        summed[5],
        summed[6],
        summed[7],
    )


def solution(mesh):
    return jax.shard_map(
        body,
        mesh=mesh,
        in_specs=(
            P("seq", "tok", None),
            P("seq", "tok", None),
            P("seq", None),
            P("seq"),
            P("tok", "seq"),
            P("tok", "seq"),
            P("tok", "seq"),
            P("tok", "seq"),
            P("tok"),
            P("tok"),
            P(),
            P(),
            P(),
            P(),
            P(),
            P(),
            P(),
            P(),
        ),
        out_specs=(
            P("seq", "tok", None),
            P("seq", "tok", None),
            P(),
            P(),
            P(),
            P(),
            P(),
            P(),
            P(),
            P(),
        ),
        check_vma=False,
    )
```

profile of v0, /device:TPU:0, one launch (start us, length us, event | category | flops | bytes accessed | tf_op | source)
XLA Modules:
  0.0 1193.3 jit_solution(8519961414103918297)
XLA Ops:
  7.3 11.8 all_gather.45
  44.1 75.4 %all-gather.10.cloned.1.call-done = bf16[1024,3072]{1,0:T(8,128)(2,1)} async-done(((bf16[1024,384]{1,0:T(8,128)(2,1)}), bf16[1024,3072]{1,0:T(8,128)(2,1)}) %all-gather.10.cloned.1.call-update) | async-done | bytes 6291472 | tf_op jit(solution)/shard_map/all_gather | solution.py:150
  169.6 59.1 %all-gather.22.cloned.1.call-done = bf16[2624,1024]{1,0:T(8,128)(2,1)} async-done(((bf16[2624,128]{1,0:T(8,128)(2,1)}), bf16[2624,1024]{1,0:T(8,128)(2,1)}) %all-gather.22.cloned.1.call-update) | async-done | bytes 5373968 | tf_op jit(solution)/shard_map/all_gather | solution.py:153
  236.1 15.5 %all-gather.14.cloned.1.call-done = bf16[1,1024,1024]{2,1,0:T(8,128)(2,1)} async-done(((bf16[1,256,1024]{2,1,0:T(8,128)(2,1)}), bf16[1,1024,1024]{2,1,0:T(8,128)(2,1)}) %all-gather.14.cloned.1.call-update) | async-done | bytes 2097168 | tf_op jit(solution)/shard_map/all_gather | solution.py:174
  255.5 20.6 %all-gather.12.cloned.1.call-done = bf16[1,1024,1024]{2,1,0:T(8,128)(2,1)} async-done(((bf16[1,256,1024]{2,1,0:T(8,128)(2,1)}), bf16[1,1024,1024]{2,1,0:T(8,128)(2,1)}) %all-gather.12.cloned.1.call-update) | async-done | bytes 2097168 | tf_op jit(solution)/shard_map/all_gather | solution.py:175
  280.1 45.8 %while.30 = (s32[]{:T(128)}, bf16[8,1,256,128]{2,3,1,0:T(8,128)(2,1)S(1)}, f32[8,1,2,256]{3,2,1,0:T(2,128)}, s32[8]{0:T(128)S(1)}, bf16[1,1024,1024]{1,2,0:T(8,1...) while((s32[]{:T(128)}, ...), condition=%wide.region_5.6_spmd.clone.clone, body=%wide.region_2.5_spmd.clone.sunk.clone | while | flops 138149376 | bytes 8804011 | solution.py:192
  332.7 151.0 %all-gather.20.cloned.1.call-done = bf16[1024,5248]{0,1:T(8,128)(2,1)} async-done(((bf16[1024,656]{0,1:T(8,128)(2,1)}), bf16[1024,5248]{0,1:T(8,128)(2,1)}) %all-gather.20.cloned.1.call-update) | async-done | bytes 10747920 | tf_op jit(solution)/shard_map/all_gather | solution.py:152
  511.9 468.5 %while.31 = (s32[]{:T(128)}, f32[8,1,256,128]{2,3,1,0:T(8,128)}, f32[8,1,256,128]{2,3,1,0:T(8,128)}, bf16[8,1,256,128]{2,3,1,0:T(8,128)(2,1)}, s32[8]{0:T(128)S(...) while((s32[]{:T(128)}, f32[8,1,256,128]{2,3,1,0:T(8,128)}, ...), condition=%wide.region_14.15_spmd.clone.clone, body=%wide.region_10.14_spmd.clone.sunk.clone | while | flops 343477248 | bytes 23342488 | solution.py:284
  546.3 21.2 %reduce-scatter.5.cloned.1.call-done = bf16[1,256,128]{1,2,0:T(8,128)(2,1)} async-done(((bf16[1,1024,128]{1,2,0:T(8,128)(2,1)}), bf16[1,256,128]{1,2,0:T(8,128)(2,1)}) %reduce-scatter.5.cloned.1.call-update) | async-done | bytes 65552 | tf_op jit(solution)/shard_map/while/body/eval_jaxpr/reduce_scatter | solution.py:275
  591.2 12.4 %reduce-scatter.3.cloned.1.call-done = bf16[1,256,128]{1,2,0:T(8,128)(2,1)} async-done(((bf16[1,1024,128]{1,2,0:T(8,128)(2,1)}), bf16[1,256,128]{1,2,0:T(8,128)(2,1)}) %reduce-scatter.3.cloned.1.call-update) | async-done | bytes 65552 | tf_op jit(solution)/shard_map/while/body/eval_jaxpr/reduce_scatter | solution.py:269
  605.1 21.1 %reduce-scatter.5.cloned.1.call-done = bf16[1,256,128]{1,2,0:T(8,128)(2,1)} async-done(((bf16[1,1024,128]{1,2,0:T(8,128)(2,1)}), bf16[1,256,128]{1,2,0:T(8,128)(2,1)}) %reduce-scatter.5.cloned.1.call-update) | async-done | bytes 65552 | tf_op jit(solution)/shard_map/while/body/eval_jaxpr/reduce_scatter | solution.py:275
  650.0 12.4 %reduce-scatter.3.cloned.1.call-done = bf16[1,256,128]{1,2,0:T(8,128)(2,1)} async-done(((bf16[1,1024,128]{1,2,0:T(8,128)(2,1)}), bf16[1,256,128]{1,2,0:T(8,128)(2,1)}) %reduce-scatter.3.cloned.1.call-update) | async-done | bytes 65552 | tf_op jit(solution)/shard_map/while/body/eval_jaxpr/reduce_scatter | solution.py:269
  663.9 21.1 %reduce-scatter.5.cloned.1.call-done = bf16[1,256,128]{1,2,0:T(8,128)(2,1)} async-done(((bf16[1,1024,128]{1,2,0:T(8,128)(2,1)}), bf16[1,256,128]{1,2,0:T(8,128)(2,1)}) %reduce-scatter.5.cloned.1.call-update) | async-done | bytes 65552 | tf_op jit(solution)/shard_map/while/body/eval_jaxpr/reduce_scatter | solution.py:275
  708.8 12.4 %reduce-scatter.3.cloned.1.call-done = bf16[1,256,128]{1,2,0:T(8,128)(2,1)} async-done(((bf16[1,1024,128]{1,2,0:T(8,128)(2,1)}), bf16[1,256,128]{1,2,0:T(8,128)(2,1)}) %reduce-scatter.3.cloned.1.call-update) | async-done | bytes 65552 | tf_op jit(solution)/shard_map/while/body/eval_jaxpr/reduce_scatter | solution.py:269
  722.7 21.0 %reduce-scatter.5.cloned.1.call-done = bf16[1,256,128]{1,2,0:T(8,128)(2,1)} async-done(((bf16[1,1024,128]{1,2,0:T(8,128)(2,1)}), bf16[1,256,128]{1,2,0:T(8,128)(2,1)}) %reduce-scatter.5.cloned.1.call-update) | async-done | bytes 65552 | tf_op jit(solution)/shard_map/while/body/eval_jaxpr/reduce_scatter | solution.py:275
  767.4 12.4 %reduce-scatter.3.cloned.1.call-done = bf16[1,256,128]{1,2,0:T(8,128)(2,1)} async-done(((bf16[1,1024,128]{1,2,0:T(8,128)(2,1)}), bf16[1,256,128]{1,2,0:T(8,128)(2,1)}) %reduce-scatter.3.cloned.1.call-update) | async-done | bytes 65552 | tf_op jit(solution)/shard_map/while/body/eval_jaxpr/reduce_scatter | solution.py:269
  781.4 21.0 %reduce-scatter.5.cloned.1.call-done = bf16[1,256,128]{1,2,0:T(8,128)(2,1)} async-done(((bf16[1,1024,128]{1,2,0:T(8,128)(2,1)}), bf16[1,256,128]{1,2,0:T(8,128)(2,1)}) %reduce-scatter.5.cloned.1.call-update) | async-done | bytes 65552 | tf_op jit(solution)/shard_map/while/body/eval_jaxpr/reduce_scatter | solution.py:275
  826.2 12.4 %reduce-scatter.3.cloned.1.call-done = bf16[1,256,128]{1,2,0:T(8,128)(2,1)} async-done(((bf16[1,1024,128]{1,2,0:T(8,128)(2,1)}), bf16[1,256,128]{1,2,0:T(8,128)(2,1)}) %reduce-scatter.3.cloned.1.call-update) | async-done | bytes 65552 | tf_op jit(solution)/shard_map/while/body/eval_jaxpr/reduce_scatter | solution.py:269
  840.1 21.2 %reduce-scatter.5.cloned.1.call-done = bf16[1,256,128]{1,2,0:T(8,128)(2,1)} async-done(((bf16[1,1024,128]{1,2,0:T(8,128)(2,1)}), bf16[1,256,128]{1,2,0:T(8,128)(2,1)}) %reduce-scatter.5.cloned.1.call-update) | async-done | bytes 65552 | tf_op jit(solution)/shard_map/while/body/eval_jaxpr/reduce_scatter | solution.py:275
  884.9 12.4 %reduce-scatter.3.cloned.1.call-done = bf16[1,256,128]{1,2,0:T(8,128)(2,1)} async-done(((bf16[1,1024,128]{1,2,0:T(8,128)(2,1)}), bf16[1,256,128]{1,2,0:T(8,128)(2,1)}) %reduce-scatter.3.cloned.1.call-update) | async-done | bytes 65552 | tf_op jit(solution)/shard_map/while/body/eval_jaxpr/reduce_scatter | solution.py:269
  898.9 21.2 %reduce-scatter.5.cloned.1.call-done = bf16[1,256,128]{1,2,0:T(8,128)(2,1)} async-done(((bf16[1,1024,128]{1,2,0:T(8,128)(2,1)}), bf16[1,256,128]{1,2,0:T(8,128)(2,1)}) %reduce-scatter.5.cloned.1.call-update) | async-done | bytes 65552 | tf_op jit(solution)/shard_map/while/body/eval_jaxpr/reduce_scatter | solution.py:275
  943.8 12.4 %reduce-scatter.3.cloned.1.call-done = bf16[1,256,128]{1,2,0:T(8,128)(2,1)} async-done(((bf16[1,1024,128]{1,2,0:T(8,128)(2,1)}), bf16[1,256,128]{1,2,0:T(8,128)(2,1)}) %reduce-scatter.3.cloned.1.call-update) | async-done | bytes 65552 | tf_op jit(solution)/shard_map/while/body/eval_jaxpr/reduce_scatter | solution.py:269
  957.7 21.2 %reduce-scatter.5.cloned.1.call-done = bf16[1,256,128]{1,2,0:T(8,128)(2,1)} async-done(((bf16[1,1024,128]{1,2,0:T(8,128)(2,1)}), bf16[1,256,128]{1,2,0:T(8,128)(2,1)}) %reduce-scatter.5.cloned.1.call-update) | async-done | bytes 65552 | tf_op jit(solution)/shard_map/while/body/eval_jaxpr/reduce_scatter | solution.py:275
  1007.6 166.9 %all-reduce.7.cloned.1.call-done = (f32[8,16,1024]{2,1,0:T(8,128)}, f32[8,16,3072]{2,1,0:T(8,128)}, f32[8,16,1024]{2,1,0:T(8,128)}, f32[8,16,1024]{2,1,0:T(8,128...) async-done(((f32[8,16,1024]{2,1,0:T(8,128)}, f32[8,16,3072]{2,1,0:T(8,128)}, f32[8,16,1024]{2,1,0:T(8,128)}, ...) | async-done | bytes 8224784 | tf_op jit(solution)/shard_map/psum | solution.py:304
  (517 shorter events, 394.1 us)
Async XLA Ops:
  7.2 112.3 %all-gather.10.cloned.1.call-start = ((), (), s32[]{:S(2)}) async-start(), calls=%async_computation.2 | async-start | bytes 7077888 | tf_op jit(solution)/shard_map/all_gather | solution.py:150
  19.1 136.7 %all-gather.18.cloned.1.call-start = ((), (), s32[]{:S(2)}) async-start(), calls=%async_computation.6 | async-start | bytes 1679360 | tf_op jit(solution)/shard_map/all_gather | solution.py:144
  19.8 208.9 %all-gather.22.cloned.1.call-start = ((), (), s32[]{:S(2)}) async-start(), calls=%async_computation.8 | async-start | bytes 6045696 | tf_op jit(solution)/shard_map/all_gather | solution.py:153
  28.6 222.9 %all-gather.14.cloned.1.call-start = ((), (), s32[]{:S(2)}) async-start(), calls=%async_computation.4 | async-start | bytes 2621440 | tf_op jit(solution)/shard_map/all_gather | solution.py:174
  146.9 129.2 %all-gather.12.cloned.1.call-start = ((), (), s32[]{:S(2)}) async-start(), calls=%async_computation.3 | async-start | bytes 2621440 | tf_op jit(solution)/shard_map/all_gather | solution.py:175
  149.3 179.9 %all-gather.16.cloned.1.call-start = ((), (), s32[]{:S(2)}) async-start(), calls=%async_computation.5 | async-start | bytes 2359296 | tf_op jit(solution)/shard_map/all_gather | solution.py:151
  155.7 327.9 %all-gather.20.cloned.1.call-start = ((), (), s32[]{:S(2)}) async-start(), calls=%async_computation.7 | async-start | bytes 12091392 | tf_op jit(solution)/shard_map/all_gather | solution.py:152
  511.9 32.9 %reduce-scatter.3.cloned.1.call-start = ((), (), s32[]{:S(2)}) async-start(), calls=%async_computation.10 | async-start | bytes 327680 | tf_op jit(solution)/shard_map/while/body/eval_jaxpr/reduce_scatter | solution.py:269
  526.4 41.0 %reduce-scatter.5.cloned.1.call-start = ((), (), s32[]{:S(2)}) async-start(), calls=%async_computation.11 | async-start | bytes 327680 | tf_op jit(solution)/shard_map/while/body/eval_jaxpr/reduce_scatter | solution.py:275
  568.9 34.7 %reduce-scatter.3.cloned.1.call-start = ((), (), s32[]{:S(2)}) async-start(), calls=%async_computation.10 | async-start | bytes 327680 | tf_op jit(solution)/shard_map/while/body/eval_jaxpr/reduce_scatter | solution.py:269
  583.4 42.8 %reduce-scatter.5.cloned.1.call-start = ((), (), s32[]{:S(2)}) async-start(), calls=%async_computation.11 | async-start | bytes 327680 | tf_op jit(solution)/shard_map/while/body/eval_jaxpr/reduce_scatter | solution.py:275
  627.7 34.7 %reduce-scatter.3.cloned.1.call-start = ((), (), s32[]{:S(2)}) async-start(), calls=%async_computation.10 | async-start | bytes 327680 | tf_op jit(solution)/shard_map/while/body/eval_jaxpr/reduce_scatter | solution.py:269
  642.2 42.8 %reduce-scatter.5.cloned.1.call-start = ((), (), s32[]{:S(2)}) async-start(), calls=%async_computation.11 | async-start | bytes 327680 | tf_op jit(solution)/shard_map/while/body/eval_jaxpr/reduce_scatter | solution.py:275
  686.5 34.7 %reduce-scatter.3.cloned.1.call-start = ((), (), s32[]{:S(2)}) async-start(), calls=%async_computation.10 | async-start | bytes 327680 | tf_op jit(solution)/shard_map/while/body/eval_jaxpr/reduce_scatter | solution.py:269
  701.0 42.7 %reduce-scatter.5.cloned.1.call-start = ((), (), s32[]{:S(2)}) async-start(), calls=%async_computation.11 | async-start | bytes 327680 | tf_op jit(solution)/shard_map/while/body/eval_jaxpr/reduce_scatter | solution.py:275
  745.2 34.7 %reduce-scatter.3.cloned.1.call-start = ((), (), s32[]{:S(2)}) async-start(), calls=%async_computation.10 | async-start | bytes 327680 | tf_op jit(solution)/shard_map/while/body/eval_jaxpr/reduce_scatter | solution.py:269
  759.6 42.8 %reduce-scatter.5.cloned.1.call-start = ((), (), s32[]{:S(2)}) async-start(), calls=%async_computation.11 | async-start | bytes 327680 | tf_op jit(solution)/shard_map/while/body/eval_jaxpr/reduce_scatter | solution.py:275
  803.9 34.7 %reduce-scatter.3.cloned.1.call-start = ((), (), s32[]{:S(2)}) async-start(), calls=%async_computation.10 | async-start | bytes 327680 | tf_op jit(solution)/shard_map/while/body/eval_jaxpr/reduce_scatter | solution.py:269
  818.4 42.9 %reduce-scatter.5.cloned.1.call-start = ((), (), s32[]{:S(2)}) async-start(), calls=%async_computation.11 | async-start | bytes 327680 | tf_op jit(solution)/shard_map/while/body/eval_jaxpr/reduce_scatter | solution.py:275
  862.7 34.6 %reduce-scatter.3.cloned.1.call-start = ((), (), s32[]{:S(2)}) async-start(), calls=%async_computation.10 | async-start | bytes 327680 | tf_op jit(solution)/shard_map/while/body/eval_jaxpr/reduce_scatter | solution.py:269
  877.2 42.9 %reduce-scatter.5.cloned.1.call-start = ((), (), s32[]{:S(2)}) async-start(), calls=%async_computation.11 | async-start | bytes 327680 | tf_op jit(solution)/shard_map/while/body/eval_jaxpr/reduce_scatter | solution.py:275
  921.5 34.7 %reduce-scatter.3.cloned.1.call-start = ((), (), s32[]{:S(2)}) async-start(), calls=%async_computation.10 | async-start | bytes 327680 | tf_op jit(solution)/shard_map/while/body/eval_jaxpr/reduce_scatter | solution.py:269
  936.0 42.9 %reduce-scatter.5.cloned.1.call-start = ((), (), s32[]{:S(2)}) async-start(), calls=%async_computation.11 | async-start | bytes 327680 | tf_op jit(solution)/shard_map/while/body/eval_jaxpr/reduce_scatter | solution.py:275
  980.4 194.1 %all-reduce.7.cloned.1.call-start = ((), (), s32[]{:S(2)}) async-start(), calls=%async_computation.9 | async-start | bytes 16515072 | tf_op jit(solution)/shard_map/psum | solution.py:304
  (80 other events, 676.5 us)
Sparse Core Ops, SparseCore 0:
  19.2 100.2 all-gather.9
  121.1 16.6 all-gather.17
  139.8 88.8 all-gather.21
  230.7 20.7 all-gather.13
  253.5 22.5 all-gather.11
  278.0 51.1 all-gather.15
  331.4 152.2 all-gather.19
  526.5 18.2 reduce-scatter.2
  547.4 19.9 reduce-scatter.4
  583.5 20.0 reduce-scatter.2
  606.2 19.9 reduce-scatter.4
  642.3 20.0 reduce-scatter.2
  665.0 19.9 reduce-scatter.4
  701.1 20.0 reduce-scatter.2
  723.7 20.0 reduce-scatter.4
  759.8 20.0 reduce-scatter.2
  782.3 20.0 reduce-scatter.4
  818.5 20.0 reduce-scatter.2
  841.2 20.0 reduce-scatter.4
  877.3 20.0 reduce-scatter.2
  900.0 20.0 reduce-scatter.4
  936.1 20.0 reduce-scatter.2
  958.8 20.0 reduce-scatter.4
  994.2 180.2 all-reduce.6
where the time goes:
time: 1200 us; the launch traced here: 1190 us
  waiting for transfers between devices  760 us (63%)
  matrix products  161 us (13%)
  local copies, waits for them, and re-layouts  125 us (10%)
  other arithmetic  65.6 us (5%)
  blocking collectives  37.7 us (3%)
  loops' own time  27.1 us (2%)
  between operations  15.8 us (1%)
    reduce_scatter x8, waiting for transfers between devices, summed_group(): lax.psum_scatter(grad_value.reshape(seq_count, seq_length, group_width).a...  169 us
    psum x1, waiting for transfers between devices, body(): lax.psum((spread_back(terms[0], onehot), spread_back(terms[1], onehot), s...  167 us
    all_gather x1, waiting for transfers between devices, body(): lax.all_gather(tok_parts[2], 'seq', axis=1, tiled=True)  151 us
    reduce_scatter x8, waiting for transfers between devices, summed_group(): lax.psum_scatter(grad_key.reshape(seq_count, seq_length, group_width).ast...  97.5 us
    all_gather x1, waiting for transfers between devices, body(): lax.all_gather(tok_parts[0], 'seq', axis=1, tiled=True)  75.4 us
    all_gather x1, waiting for transfers between devices, body(): lax.all_gather(tok_parts[3], 'seq', axis=1, tiled=True)  59.1 us
    dynamic_slice x48, local copies, waits for them, and re-layouts, heads_slice(): lax.dynamic_slice_in_dim(source, group_index * group_width, group_width, 2)  48.9 us
    dot_general x8, matrix products, summed_group(): jnp.einsum('shqk,sqhd->skhd', grad_scores, query_part, preferred_element_...  28.5 us
  transfers between devices with their start and end apart: 24, of which 23 were waited for; matrix products, arithmetic and copies ran while one was open for 16% of the time, Pallas kernels for 0%

commit v1 on v0

--- a/solution.py
+++ b/solution.py
@@ -302,17 +302,20 @@
     input_grad = (grad_mid + norm_one_back(back_norm_one)[0]).astype(jnp.bfloat16)
     terms = (down_qkv, up_qkv, down_out, up_out, down_in, up_in, down_o2, up_o2)
     summed = lax.psum(
-        (
-            spread_back(terms[0], onehot),
-            spread_back(terms[1], onehot),
-            spread_back(terms[2], onehot),
-            spread_back(terms[3], onehot),
-            spread_back(terms[4], onehot),
-            spread_back(terms[5], onehot),
-            spread_back(terms[6], onehot),
-            spread_back(terms[7], onehot),
+        lax.psum(
+            (
+                spread_back(terms[0], onehot),
+                spread_back(terms[1], onehot),
+                spread_back(terms[2], onehot),
+                spread_back(terms[3], onehot),
+                spread_back(terms[4], onehot),
+                spread_back(terms[5], onehot),
+                spread_back(terms[6], onehot),
+                spread_back(terms[7], onehot),
+            ),
+            "tok",
         ),
-        ("seq", "tok"),
+        "seq",
     )
     return (
         layer_out,

time: 1200 us -> 1450 us (1.21)
  waiting for transfers between devices: 760 us -> 1010 us
    psum x0 -> x1, waiting for transfers between devices: none -> 264 us  [body(): lax.psum(lax.psum((spread_back(terms[0], onehot), spread_back(terms[1], o...]
  transfers between devices with their start and end apart: 24 -> 25, of which waited for: 23 -> 24; matrix products, arithmetic and copies ran while one was open for 16% -> 13% of each run, Pallas kernels for 0% -> 0%
where the time goes in v1:
time: 1450 us; the launch traced here: 1440 us
  waiting for transfers between devices  1010 us (70%)
  matrix products  161 us (11%)
  local copies, waits for them, and re-layouts  125 us (9%)
  other arithmetic  65.6 us (5%)
  blocking collectives  37.7 us (3%)
  loops' own time  27.1 us (2%)
  between operations  15.5 us (1%)
    psum x1, waiting for transfers between devices, body(): lax.psum(lax.psum((spread_back(terms[0], onehot), spread_back(terms[1], o...  264 us
    reduce_scatter x8, waiting for transfers between devices, summed_group(): lax.psum_scatter(grad_value.reshape(seq_count, seq_length, group_width).a...  169 us
    psum x1, waiting for transfers between devices, body(): lax.psum((spread_back(terms[0], onehot), spread_back(terms[1], onehot), s...  153 us
    all_gather x1, waiting for transfers between devices, body(): lax.all_gather(tok_parts[2], 'seq', axis=1, tiled=True)  151 us
    reduce_scatter x8, waiting for transfers between devices, summed_group(): lax.psum_scatter(grad_key.reshape(seq_count, seq_length, group_width).ast...  96.9 us
    all_gather x1, waiting for transfers between devices, body(): lax.all_gather(tok_parts[0], 'seq', axis=1, tiled=True)  75.4 us
    all_gather x1, waiting for transfers between devices, body(): lax.all_gather(tok_parts[3], 'seq', axis=1, tiled=True)  59.1 us
    dynamic_slice x48, local copies, waits for them, and re-layouts, heads_slice(): lax.dynamic_slice_in_dim(source, group_index * group_width, group_width, 2)  48.8 us
  transfers between devices with their start and end apart: 25, of which 24 were waited for; matrix products, arithmetic and copies ran while one was open for 13% of the time, Pallas kernels for 0%

profile of v1, /device:TPU:0, one launch (start us, length us, event | category | flops | bytes accessed | tf_op | source)
XLA Modules:
  0.0 1442.7 jit_solution(8183967225230349632)
XLA Ops:
  44.1 75.4 %all-gather.10.cloned.1.call-done = bf16[1024,3072]{1,0:T(8,128)(2,1)} async-done(((bf16[1024,384]{1,0:T(8,128)(2,1)}), bf16[1024,3072]{1,0:T(8,128)(2,1)}) %all-gather.10.cloned.1.call-update) | async-done | bytes 6291472 | tf_op jit(solution)/shard_map/all_gather | solution.py:150
  169.6 59.1 %all-gather.22.cloned.1.call-done = bf16[2624,1024]{1,0:T(8,128)(2,1)} async-done(((bf16[2624,128]{1,0:T(8,128)(2,1)}), bf16[2624,1024]{1,0:T(8,128)(2,1)}) %all-gather.22.cloned.1.call-update) | async-done | bytes 5373968 | tf_op jit(solution)/shard_map/all_gather | solution.py:153
  236.1 15.5 %all-gather.14.cloned.1.call-done = bf16[1,1024,1024]{2,1,0:T(8,128)(2,1)} async-done(((bf16[1,256,1024]{2,1,0:T(8,128)(2,1)}), bf16[1,1024,1024]{2,1,0:T(8,128)(2,1)}) %all-gather.14.cloned.1.call-update) | async-done | bytes 2097168 | tf_op jit(solution)/shard_map/all_gather | solution.py:174
  255.5 20.6 %all-gather.12.cloned.1.call-done = bf16[1,1024,1024]{2,1,0:T(8,128)(2,1)} async-done(((bf16[1,256,1024]{2,1,0:T(8,128)(2,1)}), bf16[1,1024,1024]{2,1,0:T(8,128)(2,1)}) %all-gather.12.cloned.1.call-update) | async-done | bytes 2097168 | tf_op jit(solution)/shard_map/all_gather | solution.py:175
  280.1 45.8 %while.30 = (s32[]{:T(128)}, bf16[8,1,256,128]{2,3,1,0:T(8,128)(2,1)S(1)}, f32[8,1,2,256]{3,2,1,0:T(2,128)}, s32[8]{0:T(128)S(1)}, bf16[1,1024,1024]{1,2,0:T(8,1...) while((s32[]{:T(128)}, ...), condition=%wide.region_5.6_spmd.clone.clone, body=%wide.region_2.5_spmd.clone.sunk.clone | while | flops 138149376 | bytes 8804011 | solution.py:192
  332.7 151.0 %all-gather.20.cloned.1.call-done = bf16[1024,5248]{0,1:T(8,128)(2,1)} async-done(((bf16[1024,656]{0,1:T(8,128)(2,1)}), bf16[1024,5248]{0,1:T(8,128)(2,1)}) %all-gather.20.cloned.1.call-update) | async-done | bytes 10747920 | tf_op jit(solution)/shard_map/all_gather | solution.py:152
  511.9 468.2 %while.31 = (s32[]{:T(128)}, f32[8,1,256,128]{2,3,1,0:T(8,128)}, f32[8,1,256,128]{2,3,1,0:T(8,128)}, bf16[8,1,256,128]{2,3,1,0:T(8,128)(2,1)}, s32[8]{0:T(128)S(...) while((s32[]{:T(128)}, f32[8,1,256,128]{2,3,1,0:T(8,128)}, ...), condition=%wide.region_14.15_spmd.clone.clone, body=%wide.region_10.14_spmd.clone.sunk.clone | while | flops 343477248 | bytes 23342488 | solution.py:284
  546.2 21.2 %reduce-scatter.5.cloned.1.call-done = bf16[1,256,128]{1,2,0:T(8,128)(2,1)} async-done(((bf16[1,1024,128]{1,2,0:T(8,128)(2,1)}), bf16[1,256,128]{1,2,0:T(8,128)(2,1)}) %reduce-scatter.5.cloned.1.call-update) | async-done | bytes 65552 | tf_op jit(solution)/shard_map/while/body/eval_jaxpr/reduce_scatter | solution.py:275
  591.2 12.3 reduce-scatter.3.cloned.1.call-done
  605.0 21.2 %reduce-scatter.5.cloned.1.call-done = bf16[1,256,128]{1,2,0:T(8,128)(2,1)} async-done(((bf16[1,1024,128]{1,2,0:T(8,128)(2,1)}), bf16[1,256,128]{1,2,0:T(8,128)(2,1)}) %reduce-scatter.5.cloned.1.call-update) | async-done | bytes 65552 | tf_op jit(solution)/shard_map/while/body/eval_jaxpr/reduce_scatter | solution.py:275
  650.0 12.3 reduce-scatter.3.cloned.1.call-done
  663.8 21.2 %reduce-scatter.5.cloned.1.call-done = bf16[1,256,128]{1,2,0:T(8,128)(2,1)} async-done(((bf16[1,1024,128]{1,2,0:T(8,128)(2,1)}), bf16[1,256,128]{1,2,0:T(8,128)(2,1)}) %reduce-scatter.5.cloned.1.call-update) | async-done | bytes 65552 | tf_op jit(solution)/shard_map/while/body/eval_jaxpr/reduce_scatter | solution.py:275
  708.8 12.3 reduce-scatter.3.cloned.1.call-done
  722.6 21.0 %reduce-scatter.5.cloned.1.call-done = bf16[1,256,128]{1,2,0:T(8,128)(2,1)} async-done(((bf16[1,1024,128]{1,2,0:T(8,128)(2,1)}), bf16[1,256,128]{1,2,0:T(8,128)(2,1)}) %reduce-scatter.5.cloned.1.call-update) | async-done | bytes 65552 | tf_op jit(solution)/shard_map/while/body/eval_jaxpr/reduce_scatter | solution.py:275
  767.4 12.3 reduce-scatter.3.cloned.1.call-done
  781.3 21.0 %reduce-scatter.5.cloned.1.call-done = bf16[1,256,128]{1,2,0:T(8,128)(2,1)} async-done(((bf16[1,1024,128]{1,2,0:T(8,128)(2,1)}), bf16[1,256,128]{1,2,0:T(8,128)(2,1)}) %reduce-scatter.5.cloned.1.call-update) | async-done | bytes 65552 | tf_op jit(solution)/shard_map/while/body/eval_jaxpr/reduce_scatter | solution.py:275
  826.0 12.3 reduce-scatter.3.cloned.1.call-done
  839.9 21.2 %reduce-scatter.5.cloned.1.call-done = bf16[1,256,128]{1,2,0:T(8,128)(2,1)} async-done(((bf16[1,1024,128]{1,2,0:T(8,128)(2,1)}), bf16[1,256,128]{1,2,0:T(8,128)(2,1)}) %reduce-scatter.5.cloned.1.call-update) | async-done | bytes 65552 | tf_op jit(solution)/shard_map/while/body/eval_jaxpr/reduce_scatter | solution.py:275
  884.8 12.3 reduce-scatter.3.cloned.1.call-done
  898.7 21.2 %reduce-scatter.5.cloned.1.call-done = bf16[1,256,128]{1,2,0:T(8,128)(2,1)} async-done(((bf16[1,1024,128]{1,2,0:T(8,128)(2,1)}), bf16[1,256,128]{1,2,0:T(8,128)(2,1)}) %reduce-scatter.5.cloned.1.call-update) | async-done | bytes 65552 | tf_op jit(solution)/shard_map/while/body/eval_jaxpr/reduce_scatter | solution.py:275
  943.6 12.3 reduce-scatter.3.cloned.1.call-done
  957.4 21.2 %reduce-scatter.5.cloned.1.call-done = bf16[1,256,128]{1,2,0:T(8,128)(2,1)} async-done(((bf16[1,1024,128]{1,2,0:T(8,128)(2,1)}), bf16[1,256,128]{1,2,0:T(8,128)(2,1)}) %reduce-scatter.5.cloned.1.call-update) | async-done | bytes 65552 | tf_op jit(solution)/shard_map/while/body/eval_jaxpr/reduce_scatter | solution.py:275
  993.8 153.1 %all-reduce.11.cloned.1.call-done = (f32[8,16,1024]{2,1,0:T(8,128)}, f32[8,16,3072]{2,1,0:T(8,128)}, f32[8,16,1024]{2,1,0:T(8,128)}, f32[8,16,1024]{2,1,0:T(8,12...) async-done(((f32[8,16,1024]{2,1,0:T(8,128)}, f32[8,16,3072]{2,1,0:T(8,128)}, f32[8,16,1024]{2,1,0:T(8,128)}, ...) | async-done | bytes 8224784 | tf_op jit(solution)/shard_map/psum | solution.py:305
  1160.0 264.2 %all-reduce.9.cloned.1.call-done = (f32[8,16,1024]{2,1,0:T(8,128)}, f32[8,16,3072]{2,1,0:T(8,128)}, f32[8,16,1024]{2,1,0:T(8,128)}, f32[8,16,1024]{2,1,0:T(8,128...) async-done(((f32[8,16,1024]{2,1,0:T(8,128)}, f32[8,16,3072]{2,1,0:T(8,128)}, f32[8,16,1024]{2,1,0:T(8,128)}, ...) | async-done | bytes 8224784 | tf_op jit(solution)/shard_map/psum | solution.py:304
  (520 shorter events, 405.6 us)
Async XLA Ops:
  7.2 112.3 %all-gather.10.cloned.1.call-start = ((), (), s32[]{:S(2)}) async-start(), calls=%async_computation.2 | async-start | bytes 7077888 | tf_op jit(solution)/shard_map/all_gather | solution.py:150
  19.1 136.8 %all-gather.18.cloned.1.call-start = ((), (), s32[]{:S(2)}) async-start(), calls=%async_computation.6 | async-start | bytes 1679360 | tf_op jit(solution)/shard_map/all_gather | solution.py:144
  19.8 208.9 %all-gather.22.cloned.1.call-start = ((), (), s32[]{:S(2)}) async-start(), calls=%async_computation.8 | async-start | bytes 6045696 | tf_op jit(solution)/shard_map/all_gather | solution.py:153
  28.7 222.9 %all-gather.14.cloned.1.call-start = ((), (), s32[]{:S(2)}) async-start(), calls=%async_computation.4 | async-start | bytes 2621440 | tf_op jit(solution)/shard_map/all_gather | solution.py:174
  147.0 129.2 %all-gather.12.cloned.1.call-start = ((), (), s32[]{:S(2)}) async-start(), calls=%async_computation.3 | async-start | bytes 2621440 | tf_op jit(solution)/shard_map/all_gather | solution.py:175
  149.3 179.9 %all-gather.16.cloned.1.call-start = ((), (), s32[]{:S(2)}) async-start(), calls=%async_computation.5 | async-start | bytes 2359296 | tf_op jit(solution)/shard_map/all_gather | solution.py:151
  155.8 327.9 %all-gather.20.cloned.1.call-start = ((), (), s32[]{:S(2)}) async-start(), calls=%async_computation.7 | async-start | bytes 12091392 | tf_op jit(solution)/shard_map/all_gather | solution.py:152
  526.4 41.0 %reduce-scatter.5.cloned.1.call-start = ((), (), s32[]{:S(2)}) async-start(), calls=%async_computation.12 | async-start | bytes 327680 | tf_op jit(solution)/shard_map/while/body/eval_jaxpr/reduce_scatter | solution.py:275
  568.9 34.7 %reduce-scatter.3.cloned.1.call-start = ((), (), s32[]{:S(2)}) async-start(), calls=%async_computation.11 | async-start | bytes 327680 | tf_op jit(solution)/shard_map/while/body/eval_jaxpr/reduce_scatter | solution.py:269
  583.4 42.8 %reduce-scatter.5.cloned.1.call-start = ((), (), s32[]{:S(2)}) async-start(), calls=%async_computation.12 | async-start | bytes 327680 | tf_op jit(solution)/shard_map/while/body/eval_jaxpr/reduce_scatter | solution.py:275
  627.7 34.7 %reduce-scatter.3.cloned.1.call-start = ((), (), s32[]{:S(2)}) async-start(), calls=%async_computation.11 | async-start | bytes 327680 | tf_op jit(solution)/shard_map/while/body/eval_jaxpr/reduce_scatter | solution.py:269
  642.2 42.8 %reduce-scatter.5.cloned.1.call-start = ((), (), s32[]{:S(2)}) async-start(), calls=%async_computation.12 | async-start | bytes 327680 | tf_op jit(solution)/shard_map/while/body/eval_jaxpr/reduce_scatter | solution.py:275
  686.5 34.6 %reduce-scatter.3.cloned.1.call-start = ((), (), s32[]{:S(2)}) async-start(), calls=%async_computation.11 | async-start | bytes 327680 | tf_op jit(solution)/shard_map/while/body/eval_jaxpr/reduce_scatter | solution.py:269
  701.0 42.7 %reduce-scatter.5.cloned.1.call-start = ((), (), s32[]{:S(2)}) async-start(), calls=%async_computation.12 | async-start | bytes 327680 | tf_op jit(solution)/shard_map/while/body/eval_jaxpr/reduce_scatter | solution.py:275
  745.1 34.7 %reduce-scatter.3.cloned.1.call-start = ((), (), s32[]{:S(2)}) async-start(), calls=%async_computation.11 | async-start | bytes 327680 | tf_op jit(solution)/shard_map/while/body/eval_jaxpr/reduce_scatter | solution.py:269
  759.6 42.7 %reduce-scatter.5.cloned.1.call-start = ((), (), s32[]{:S(2)}) async-start(), calls=%async_computation.12 | async-start | bytes 327680 | tf_op jit(solution)/shard_map/while/body/eval_jaxpr/reduce_scatter | solution.py:275
  803.8 34.6 %reduce-scatter.3.cloned.1.call-start = ((), (), s32[]{:S(2)}) async-start(), calls=%async_computation.11 | async-start | bytes 327680 | tf_op jit(solution)/shard_map/while/body/eval_jaxpr/reduce_scatter | solution.py:269
  818.2 42.8 %reduce-scatter.5.cloned.1.call-start = ((), (), s32[]{:S(2)}) async-start(), calls=%async_computation.12 | async-start | bytes 327680 | tf_op jit(solution)/shard_map/while/body/eval_jaxpr/reduce_scatter | solution.py:275
  862.5 34.7 %reduce-scatter.3.cloned.1.call-start = ((), (), s32[]{:S(2)}) async-start(), calls=%async_computation.11 | async-start | bytes 327680 | tf_op jit(solution)/shard_map/while/body/eval_jaxpr/reduce_scatter | solution.py:269
  877.0 42.8 %reduce-scatter.5.cloned.1.call-start = ((), (), s32[]{:S(2)}) async-start(), calls=%async_computation.12 | async-start | bytes 327680 | tf_op jit(solution)/shard_map/while/body/eval_jaxpr/reduce_scatter | solution.py:275
  921.3 34.6 %reduce-scatter.3.cloned.1.call-start = ((), (), s32[]{:S(2)}) async-start(), calls=%async_computation.11 | async-start | bytes 327680 | tf_op jit(solution)/shard_map/while/body/eval_jaxpr/reduce_scatter | solution.py:269
  935.8 42.9 %reduce-scatter.5.cloned.1.call-start = ((), (), s32[]{:S(2)}) async-start(), calls=%async_computation.12 | async-start | bytes 327680 | tf_op jit(solution)/shard_map/while/body/eval_jaxpr/reduce_scatter | solution.py:275
  980.1 166.8 %all-reduce.11.cloned.1.call-start = ((), (), s32[]{:S(2)}) async-start(), calls=%async_computation.10 | async-start | bytes 16515072 | tf_op jit(solution)/shard_map/psum | solution.py:305
  993.6 430.7 %all-reduce.9.cloned.1.call-start = ((), (), s32[]{:S(2)}) async-start(), calls=%async_computation.9 | async-start | bytes 16515072 | tf_op jit(solution)/shard_map/psum | solution.py:304
  (81 other events, 709.0 us)
Sparse Core Ops, SparseCore 0:
  19.2 100.2 all-gather.9
  139.9 88.8 all-gather.21
  230.7 20.7 all-gather.13
  253.5 22.5 all-gather.11
  278.0 51.0 all-gather.15
  331.4 152.2 all-gather.19
  526.5 18.1 reduce-scatter.2
  547.3 20.0 reduce-scatter.4
  583.5 19.9 reduce-scatter.2
  606.1 20.0 reduce-scatter.4
  642.3 19.9 reduce-scatter.2
  664.9 20.0 reduce-scatter.4
  701.1 19.9 reduce-scatter.2
  723.6 20.0 reduce-scatter.4
  759.7 19.9 reduce-scatter.2
  782.2 20.0 reduce-scatter.4
  818.3 19.9 reduce-scatter.2
  841.0 20.0 reduce-scatter.4
  877.1 19.9 reduce-scatter.2
  899.8 20.0 reduce-scatter.4
  935.9 19.9 reduce-scatter.2
  958.5 20.0 reduce-scatter.4
  993.7 153.1 all-reduce.10
  1153.2 271.0 all-reduce.8
  (1 shorter events, 16.6 us)
